TPU v7x, 32 devices: a whole 2x2x4 slice. The times are simulated.
32 devices in a mesh: seq: 4 (over y, x), ep: 8 (over z, core).
Axes of the slice: x: 2, y: 2, z: 4, core: 2. Of those that a mesh axis runs over, the one named last changes fastest.
Arguments:
- tokens: bfloat16 [24, 576, 768], P('ep', 'seq'), may hold values from -6 to 6
- routes: int32 [24, 576, 2], P('ep', 'seq'), may hold values from 0 to 31, all different within a row
- priority: int32 [24, 576], P('ep', 'seq'), may hold values from 0 to 431, as said below
- hires: int32 [8], P('ep'), may hold values from 0 to 3
- gain_one: float32 [768], replicated, may hold values from 0.1 to 1.9
- shift_one: float32 [768], replicated, may hold values from -1.8 to 1.8
- w_qkv: bfloat16 [768, 2304], replicated, may hold values from -0.21875 to 0.21875
- w_proj: bfloat16 [768, 768], replicated, may hold values from -6 to 6
- gain_two: float32 [768], replicated, may hold values from 0.1 to 1.9
- shift_two: float32 [768], replicated, may hold values from -1.8 to 1.8
- w_router: bfloat16 [768, 32], replicated, may hold values from -0.15917969 to 0.15917969
- expert_in: bfloat16 [98304, 768], P('ep'), may hold values from -0.21875 to 0.21875
- expert_out: bfloat16 [98304, 768], P('ep'), may hold values from -2.5 to 2.5
- cotangent: bfloat16 [24, 576, 768], P('ep', 'seq'), may hold values from -6 to 6
Outputs:
- output: bfloat16 [24, 576, 768], P('ep', 'seq')
- input_grad: bfloat16 [24, 576, 768], P('ep', 'seq')
- gain_one_grad: float32 [768], replicated
- shift_one_grad: float32 [768], replicated
- qkv_grad: float32 [768, 2304], replicated
- proj_grad: float32 [768, 768], replicated
- gain_two_grad: float32 [768], replicated
- shift_two_grad: float32 [768], replicated
- router_grad: float32 [768, 32], replicated
- expert_in_grad: float32 [98304, 768], P('ep')
- expert_out_grad: float32 [98304, 768], P('ep')
- rms_stats: float32 [3], replicated
Inputs may be any that keep to these rules, and one draw needn't show every extreme that they name: `priority`: within each device block of 3 images times 144 positions, the priorities are a permutation of 0 to 431.
All inputs are finite; a program needn't handle non-finite values.
Results may differ from a plain program's by a relative error of at most 0.015.
Values may be sent and summed in bfloat16 or wider, within the bound.
No kernel may reach another device: no remote copies, remote signals or barrier semaphores. Data moves between devices by JAX's collectives and lax.ppermute only.
A program may use at most 320 MiB of HBM per device.

v0:
```python
import jax
import jax.numpy as jnp
from jax import lax
from jax.sharding import PartitionSpec as P

HEADS = 12
EXPERTS = 32
TOP = 2
PATCHES = 576
SHORT = 196


norm_eps = 1e-06
neg_big = -1e30


def norm_forward(values, norm_gain, norm_bias):
    row_mean = jnp.mean(values, axis=-1, keepdims=True)
    centred = values - row_mean
    inv_root = lax.rsqrt(jnp.mean(centred * centred, axis=-1, keepdims=True) + norm_eps)
    normed = centred * inv_root
    return (normed * norm_gain + norm_bias, normed, inv_root)


def norm_backward(grad_out, normed, inv_root, norm_gain):
    gain_grad = jnp.sum(grad_out * normed, axis=0)
    bias_grad = jnp.sum(grad_out, axis=0)
    scaled = grad_out * norm_gain
    grad_in = inv_root * (
        scaled
        - jnp.mean(scaled, axis=-1, keepdims=True)
        - normed * jnp.mean(scaled * normed, axis=-1, keepdims=True)
    )
    return (grad_in, gain_grad, bias_grad)


def gelu_slope(values):
    return (
        0.5 * (1.0 + lax.erf(values * 0.7071067811865476))
        + values * jnp.exp(-0.5 * values * values) * 0.3989422804014327
    )


def routing(route_rows, priority_rows, row_valid, capacity):
    row_total = route_rows.shape[0]
    by_priority = (
        jnp.zeros((row_total,), jnp.int32)
        .at[priority_rows]
        .set(jnp.arange(row_total, dtype=jnp.int32))
    )
    ordered = jnp.concatenate([route_rows[by_priority, route_rank] for route_rank in range(TOP)])
    ordered_valid = jnp.concatenate([row_valid[by_priority]] * TOP)
    expert_hits = (
        ordered[:, None] == jnp.arange(EXPERTS, dtype=jnp.int32)[None, :]
    ) & ordered_valid[:, None]
    running = jnp.cumsum(expert_hits.astype(jnp.int32), axis=0)
    ordered_slot = jnp.sum(jnp.where(expert_hits, running, 0), axis=1) - 1
    pair_slot = ordered_slot.reshape(TOP, row_total)[:, priority_rows].T
    is_kept = (pair_slot >= 0) & (pair_slot < capacity)
    return jnp.where(is_kept, route_rows * capacity + pair_slot, EXPERTS * capacity)


def slot_sources(slot_dest, fill_value, capacity, divisor):
    flat_dest = slot_dest.reshape(-1)
    source_ids = jnp.arange(flat_dest.shape[0], dtype=jnp.int32) // divisor
    table_ids = (
        jnp.full((EXPERTS * capacity + 1,), fill_value, jnp.int32).at[flat_dest].set(source_ids)
    )
    return table_ids[: EXPERTS * capacity]


def fan_out(slot_table, ep_count, split_count, local_experts, capacity):
    feature_width = slot_table.shape[-1]
    grouped = slot_table.reshape(ep_count // split_count, 1, local_experts, capacity, feature_width)
    spread = jnp.broadcast_to(
        grouped, (ep_count // split_count, split_count, local_experts, capacity, feature_width)
    )
    return spread.reshape(ep_count, local_experts, capacity, feature_width)


def fan_in(arrived, split_count):
    ep_count, local_experts, capacity, feature_width = arrived.shape
    grouped = arrived.reshape(
        ep_count // split_count, split_count, local_experts, capacity, feature_width
    )
    return jnp.sum(grouped.astype(jnp.float32), axis=1).reshape(-1, feature_width)


def score_block(query_heads, key_heads, key_mask, score_scale):
    raw_scores = (
        jnp.einsum("ishd,ithd->ihst", query_heads, key_heads, preferred_element_type=jnp.float32)
        * score_scale
    )
    return jnp.where(key_mask[:, None, None, :], raw_scores, neg_big)


def per_device(
    tokens,
    routes,
    priority,
    hires,
    gain_one,
    shift_one,
    w_qkv,
    w_proj,
    gain_two,
    shift_two,
    w_router,
    expert_in,
    expert_out,
    cotangent,
):
    image_count, patch_rows, model_width = tokens.shape
    row_count = image_count * patch_rows
    seq_count = lax.axis_size("seq")
    ep_count = lax.axis_size("ep")
    full_patches = patch_rows * seq_count
    head_width = model_width // HEADS
    score_scale = head_width ** (-0.5)
    local_experts = max(1, EXPERTS // ep_count)
    split_count = max(1, ep_count // EXPERTS)
    local_hidden = expert_in.shape[0] // local_experts
    capacity = max(2, (105 * TOP * row_count + 100 * EXPERTS - 1) // (100 * EXPERTS))
    seq_place = lax.axis_index("seq")

    def send_slots(slot_table):
        outgoing = fan_out(slot_table, ep_count, split_count, local_experts, capacity)
        return lax.all_to_all(outgoing, "ep", split_axis=0, concat_axis=0, tiled=True)

    def return_slots(part_rows):
        returned = lax.all_to_all(part_rows, "ep", split_axis=0, concat_axis=0, tiled=True)
        return fan_in(returned, split_count)

    image_length = jnp.where(jnp.arange(image_count, dtype=jnp.int32) < hires[0], PATCHES, SHORT)
    key_mask = jnp.arange(full_patches, dtype=jnp.int32)[None, :] < image_length[:, None]
    own_mask = (seq_place * patch_rows + jnp.arange(patch_rows, dtype=jnp.int32))[
        None, :
    ] < image_length[:, None]
    row_valid = own_mask.reshape(row_count)
    valid_col = row_valid.astype(jnp.float32)[:, None]
    inputs = tokens.reshape(row_count, model_width).astype(jnp.float32)
    head_shape = (image_count, -1, HEADS, head_width)
    first_out, normed_one, inv_one = norm_forward(inputs, gain_one, shift_one)
    attn_in = first_out.astype(jnp.bfloat16)
    packed = jnp.dot(attn_in, w_qkv, preferred_element_type=jnp.float32).astype(jnp.bfloat16)
    query_rows = packed[:, :model_width].reshape(image_count, patch_rows, model_width)
    key_rows = packed[:, model_width : 2 * model_width].reshape(
        image_count, patch_rows, model_width
    )
    value_rows = packed[:, 2 * model_width :].reshape(image_count, patch_rows, model_width)
    query_heads = query_rows.reshape(head_shape)
    keys_all, values_all = (
        lax.all_gather(key_rows, "seq", axis=1, tiled=True),
        lax.all_gather(value_rows, "seq", axis=1, tiled=True),
    )
    scores = score_block(query_heads, keys_all.reshape(head_shape), key_mask, score_scale)
    row_max = jnp.max(scores, axis=-1, keepdims=True)
    exp_scores = jnp.exp(scores - row_max)
    row_total = jnp.sum(exp_scores, axis=-1, keepdims=True)
    probs = exp_scores / row_total
    log_total = row_max + jnp.log(row_total)
    attended = (
        jnp.einsum(
            "ihst,ithd->ishd",
            probs.astype(jnp.bfloat16),
            values_all.reshape(head_shape),
            preferred_element_type=jnp.float32,
        )
        .reshape(row_count, model_width)
        .astype(jnp.bfloat16)
    )
    attn_out = jnp.dot(attended, w_proj, preferred_element_type=jnp.float32)
    middle = inputs + attn_out
    second_out, normed_two, inv_two = norm_forward(middle, gain_two, shift_two)
    moe_in = second_out.astype(jnp.bfloat16)
    logits = jnp.dot(moe_in, w_router, preferred_element_type=jnp.float32)
    gate_probs = jax.nn.softmax(logits, axis=-1)
    route_rows = routes.reshape(row_count, TOP)
    slot_dest = routing(route_rows, priority.reshape(row_count), row_valid, capacity)
    token_src = slot_sources(slot_dest, row_count, capacity, TOP)
    pair_src = slot_sources(slot_dest, row_count * TOP, capacity, 1)
    padded_in = jnp.concatenate([moe_in, jnp.zeros((1, model_width), jnp.bfloat16)], axis=0)
    arrived = send_slots(padded_in[token_src])
    w_first = expert_in.reshape(local_experts, local_hidden, model_width)
    w_second = expert_out.reshape(local_experts, local_hidden, model_width)
    pre_act = jnp.einsum("secd,efd->secf", arrived, w_first, preferred_element_type=jnp.float32)
    hidden = jax.nn.gelu(pre_act, approximate=False).astype(jnp.bfloat16)
    partial_out = jnp.einsum(
        "secf,efd->secd", hidden, w_second, preferred_element_type=jnp.float32
    ).astype(jnp.bfloat16)
    value_table = return_slots(partial_out)
    padded_values = jnp.concatenate([value_table, jnp.zeros((1, model_width), jnp.float32)], axis=0)
    pair_values = padded_values[slot_dest.reshape(-1)].reshape(row_count, TOP, model_width)
    chosen = jnp.take_along_axis(gate_probs, route_rows, axis=1)
    moe_out = jnp.sum(chosen[:, :, None] * pair_values, axis=1)
    total = middle + moe_out
    output = (total * valid_col).astype(jnp.bfloat16).reshape(image_count, patch_rows, model_width)
    stat_terms = jnp.stack(
        [
            jnp.sum(valid_col * attn_out * attn_out),
            jnp.sum(valid_col * moe_out * moe_out),
            jnp.sum(valid_col * total * total),
            jnp.sum(row_valid.astype(jnp.float32)) * model_width,
        ]
    )
    grad_total = cotangent.reshape(row_count, model_width).astype(jnp.float32) * valid_col
    grad_gate = jnp.sum(grad_total[:, None, :] * pair_values, axis=2)
    grad_value = (
        (grad_total[:, None, :] * chosen[:, :, None])
        .astype(jnp.bfloat16)
        .reshape(row_count * TOP, model_width)
    )
    padded_grad = jnp.concatenate([grad_value, jnp.zeros((1, model_width), jnp.bfloat16)], axis=0)
    grad_sent = send_slots(padded_grad[pair_src])
    grad_hidden = jnp.einsum(
        "secd,efd->secf", grad_sent, w_second, preferred_element_type=jnp.float32
    )
    grad_pre = (grad_hidden * gelu_slope(pre_act)).astype(jnp.bfloat16)
    grad_second = jnp.einsum(
        "secf,secd->efd", hidden, grad_sent, preferred_element_type=jnp.float32
    ).reshape(-1, model_width)
    grad_first = jnp.einsum(
        "secf,secd->efd", grad_pre, arrived, preferred_element_type=jnp.float32
    ).reshape(-1, model_width)
    grad_part_in = jnp.einsum(
        "secf,efd->secd", grad_pre, w_first, preferred_element_type=jnp.float32
    ).astype(jnp.bfloat16)
    grad_in_table = return_slots(grad_part_in)
    padded_back = jnp.concatenate([grad_in_table, jnp.zeros((1, model_width), jnp.float32)], axis=0)
    grad_dispatch = jnp.sum(
        padded_back[slot_dest.reshape(-1)].reshape(row_count, TOP, model_width), axis=1
    )
    expert_ids = jnp.arange(EXPERTS, dtype=jnp.int32)
    grad_probs = jnp.sum(
        jnp.where(route_rows[:, :, None] == expert_ids[None, None, :], grad_gate[:, :, None], 0.0),
        axis=1,
    )
    grad_logits = (
        gate_probs * (grad_probs - jnp.sum(grad_probs * gate_probs, axis=-1, keepdims=True))
    ).astype(jnp.bfloat16)
    grad_router = jnp.einsum("rd,re->de", moe_in, grad_logits, preferred_element_type=jnp.float32)
    grad_moe_in = grad_dispatch + jnp.einsum(
        "re,de->rd", grad_logits, w_router, preferred_element_type=jnp.float32
    )
    grad_mid_norm, grad_gain_two, grad_shift_two = norm_backward(
        grad_moe_in, normed_two, inv_two, gain_two
    )
    grad_middle = grad_total + grad_mid_norm
    grad_attn = grad_middle.astype(jnp.bfloat16)
    grad_proj = jnp.einsum("rd,re->de", attended, grad_attn, preferred_element_type=jnp.float32)
    grad_attended = jnp.einsum(
        "re,de->rd", grad_attn, w_proj, preferred_element_type=jnp.float32
    ).astype(jnp.bfloat16)
    grad_heads = grad_attended.reshape(head_shape)
    keys_again, values_again = (
        lax.all_gather(key_rows, "seq", axis=1, tiled=True),
        lax.all_gather(value_rows, "seq", axis=1, tiled=True),
    )
    key_heads = keys_again.reshape(head_shape)
    value_heads = values_again.reshape(head_shape)
    probs_again = jnp.exp(score_block(query_heads, key_heads, key_mask, score_scale) - log_total)
    grad_probs_att = jnp.einsum(
        "ishd,ithd->ihst", grad_heads, value_heads, preferred_element_type=jnp.float32
    )
    delta = jnp.sum(grad_probs_att * probs_again, axis=-1, keepdims=True)
    grad_scores = (probs_again * (grad_probs_att - delta)).astype(jnp.bfloat16)
    grad_queries = (
        jnp.einsum("ihst,ithd->ishd", grad_scores, key_heads, preferred_element_type=jnp.float32)
        * score_scale
    )
    grad_keys_full = (
        jnp.einsum("ihst,ishd->ithd", grad_scores, query_heads, preferred_element_type=jnp.float32)
        * score_scale
    )
    grad_values_full = jnp.einsum(
        "ihst,ishd->ithd",
        probs_again.astype(jnp.bfloat16),
        grad_heads,
        preferred_element_type=jnp.float32,
    )
    grad_keys, grad_values = (
        lax.psum_scatter(
            grad_keys_full.reshape(image_count, full_patches, model_width),
            "seq",
            scatter_dimension=1,
            tiled=True,
        ),
        lax.psum_scatter(
            grad_values_full.reshape(image_count, full_patches, model_width),
            "seq",
            scatter_dimension=1,
            tiled=True,
        ),
    )
    grad_packed = jnp.concatenate(
        [
            grad_queries.reshape(row_count, model_width),
            grad_keys.reshape(row_count, model_width),
            grad_values.reshape(row_count, model_width),
        ],
        axis=1,
    ).astype(jnp.bfloat16)
    grad_qkv = jnp.einsum("rd,re->de", attn_in, grad_packed, preferred_element_type=jnp.float32)
    grad_attn_in = jnp.einsum("re,de->rd", grad_packed, w_qkv, preferred_element_type=jnp.float32)
    grad_in_norm, grad_gain_one, grad_shift_one = norm_backward(
        grad_attn_in, normed_one, inv_one, gain_one
    )
    input_grad = (
        (grad_middle + grad_in_norm)
        .astype(jnp.bfloat16)
        .reshape(image_count, patch_rows, model_width)
    )
    summed = lax.psum(
        (
            grad_qkv,
            grad_proj,
            grad_router,
            grad_gain_one,
            grad_shift_one,
            grad_gain_two,
            grad_shift_two,
            stat_terms,
        ),
        ("seq", "ep"),
    )
    expert_grads = (
        lax.psum(grad_first.astype(jnp.bfloat16), "seq").astype(jnp.float32),
        lax.psum(grad_second.astype(jnp.bfloat16), "seq").astype(jnp.float32),
    )
    rms_stats = jnp.sqrt(summed[7][:3] / summed[7][3])
    return (
        output,
        input_grad,
        summed[3],
        summed[4],
        summed[0],
        summed[1],
        summed[5],
        summed[6],
        summed[2],
        expert_grads[0],
        expert_grads[1],
        rms_stats,
    )


def solution(mesh):
    in_specs = (
        P("ep", "seq", None),
        P("ep", "seq", None),
        P("ep", "seq"),
        P("ep"),
        P(),
        P(),
        P(),
        P(),
        P(),
        P(),
        P(),
        P("ep", None),
        P("ep", None),
        P("ep", "seq", None),
    )
    out_specs = (
        P("ep", "seq", None),
        P("ep", "seq", None),
        P(),
        P(),
        P(),
        P(),
        P(),
        P(),
        P(),
        P("ep", None),
        P("ep", None),
        P(),
    )
    return jax.shard_map(
        per_device, mesh=mesh, in_specs=in_specs, out_specs=out_specs, check_vma=False
    )
```

profile of v0, /device:TPU:0, one launch (start us, length us, event | category | flops | bytes accessed | tf_op | source)
XLA Modules:
  0.0 1413.0 jit_solution(5902060563627623308)
XLA Ops:
  28.5 6.5 gather_fusion
  35.0 7.7 gather_fusion.1
  90.7 9.3 all-gather.3.cloned.1.call-done
  105.3 8.2 fusion.37
  127.9 6.7 gather_fusion.4
  169.5 12.0 gather_fusion.8
  184.7 7.0 gather_fusion.6
  203.2 35.2 %fusion.2 = (bf16[8,4,29,3072]{3,2,0,1:T(8,128)(2,1)S(1)}, f32[4,8,29,3072]{3,2,1,0:T(8,128)}) fusion(bf16[4,3072,768,1]{2,1,3,0:T(8,128)(2,1)} %bitcast.184, bf16[8,4,29,768]{3,1,2,0:T(4,128)(2,1)} %all-to-all-done), kind=kOutput, calls=%fused_computation.24 | convolution fusion | flops 4564156416 | bytes 37404672 | tf_op jit(solution)/shard_map/secd,efd->secf/dot_general | solution.py:186
  238.3 11.5 fusion.30
  257.6 13.6 fusion.8
  271.3 11.5 fusion.31
  285.0 7.3 all-to-all-done.1
  310.3 6.7 gather_fusion.5
  321.4 7.5 multiply_reduce_fusion.1
  342.1 6.7 gather_fusion.7
  353.4 6.0 reduce_sum.241
  375.2 14.9 %multiply_reduce_fusion = (f32[3,12,144]{2,1,0:T(8,128)S(1)}, f32[3,12,144,576]{3,2,1,0:T(8,128)}) fusion(f32[3,12,144,576]{3,2,1,0:T(8,128)} %copy-done.1, f32[3,12,144]{2,1,0:T(8,128)} %log_add_fusion, bf16[3,144,12,64]{1,3,2,0:T(8,128)(2,1)} %copy.130, bf16[3,576,12,64]{1,3,2,0:T(8,128)(2,1)} %bitcast.170), kind=kOutput, calls=%fused_computation.17 | convolution fusion | flops 391158720 | bytes 27247104 | tf_op jit(solution)/shard_map/ishd,ithd->ihst/dot_general | solution.py:262
  390.1 9.9 multiply_convert_fusion
  404.7 7.5 copy.133
  412.2 9.9 fusion.25
  422.1 7.5 copy.135
  429.7 12.3 bitcast_convert_fusion
  442.0 12.1 bitcast_convert_fusion.1
  454.2 8.4 fusion.38
  478.4 61.2 %reduce-scatter.5.cloned.1.call-done = f32[3,144,768]{2,1,0:T(8,128)} async-done(((f32[3,576,768]{2,1,0:T(8,128)}), f32[3,144,768]{2,1,0:T(8,128)}) %reduce-scatter.5.cloned.1.call-update) | async-done | bytes 1327120 | tf_op jit(solution)/shard_map/reduce_scatter | solution.py:288
  541.8 6.5 fusion.42
  557.0 40.4 %all-reduce.7 = (f32[768]{0:T(1024)}, f32[768]{0:T(1024)}, f32[768]{0:T(1024)}, f32[768]{0:T(1024)}, f32[4]{0:T(128)}) all-reduce(f32[768]{0:T(1024)} %get-tuple-element.17, f32[768]{0:T(1024)} %get-tuple-element.26, f32[768]{0:T(1024)S(1)} %copy-done.36, f32[768]{0:T(1024)S(1)} %copy-done.37, ...), channel_id=1, replica_groups=mesh['seq'=4,'ep'=8] {'seq','ep'}, use_global_device_ids=true, to_apply=%region_27.28 | all-reduce | flops 3076 | bytes 24608 | tf_op jit(solution)/shard_map/psum | solution.py:313
  605.1 588.1 %all-reduce.15.cloned.1.call-done = (bf16[12288,768]{1,0:T(8,128)(2,1)}, bf16[12288,768]{1,0:T(8,128)(2,1)}) async-done(((bf16[12288,768]{1,0:T(8,128)(2,1)}, bf16[12288,768]{1,0:T(8,128)(2,1)}), (bf16[12288,768]{1,0:T(8,128)(2,1)}, bf16[12288,768]{1,0:T(8,128)(2,1)})) %all-reduce.15.cloned.1.call-update) | async-done | bytes 37748752 | tf_op jit(solution)/shard_map/psum | solution.py:327
  1193.2 21.1 %convert_element_type.149 = f32[12288,768]{1,0:T(8,128)} convert(bf16[12288,768]{1,0:T(8,128)(2,1)} %get-tuple-element.36) | non-fusion elementwise | flops 9437184 | bytes 56623104 | tf_op jit(solution)/shard_map/convert_element_type | solution.py:327
  1218.9 12.9 convert_element_type.152
  1231.8 165.5 %all-reduce.13.cloned.1.call-done = (f32[768,2304]{1,0:T(8,128)}, f32[768,768]{1,0:T(8,128)}, f32[768,32]{0,1:T(8,128)}) async-done(((f32[768,2304]{1,0:T(8,128)}, f32[768,768]{1,0:T(8,128)}, f32[768,32]{0,1:T(8,128)}), (f32[768,2304]{1,0:T(8,128)}, f32[768,768]{1,0:T(8,128)}, f32[768,32]{0,1:T(8,128)})) %all-reduce.13.cloned.1.call-update) | async-done | bytes 9535504 | tf_op jit(solution)/shard_map/psum | solution.py:313
  1397.3 6.6 copy.162
  (237 shorter events, 248.6 us)
Async XLA Ops:
  7.2 64.3 %all-gather.5.cloned.1.call-start = ((), (), s32[]{:S(2)}) async-start(), calls=%async_computation.7 | async-start | bytes 3317760 | tf_op jit(solution)/shard_map/all_gather | solution.py:153
  14.9 85.1 %all-gather.3.cloned.1.call-start = ((), (), s32[]{:S(2)}) async-start(), calls=%async_computation.6 | async-start | bytes 3317760 | tf_op jit(solution)/shard_map/all_gather | solution.py:154
  14.9 8.9 copy-start.31
  15.6 9.1 copy-start.44
  49.0 6.3 copy-start.43
  65.3 5.5 copy-start.39
  140.7 57.1 %all-to-all-start = ((bf16[8,4,29,768]{3,1,2,0:T(4,128)(2,1)}), bf16[8,4,29,768]{3,1,2,0:T(4,128)(2,1)}, u32[]{:S(2)}, u32[]{:S(2)}) async-start(bf16[8,4,29,768]{3,1,2,0:T(4,128)(2,1)} %copy.119), calls=%async_computation | async-start | bytes 2850816 | tf_op jit(solution)/shard_map/all_to_all | solution.py:128
  146.5 9.8 copy-start.25
  169.5 12.0 copy-start.38
  197.8 54.2 %all-to-all-start.2 = ((bf16[8,4,29,768]{3,1,2,0:T(4,128)(2,1)}), bf16[8,4,29,768]{3,1,2,0:T(4,128)(2,1)}, u32[]{:S(2)}, u32[]{:S(2)}) async-start(bf16[8,4,29,768]{3,1,2,0:T(4,128)(2,1)} %copy.124), calls=%async_computation.2 | async-start | bytes 2850816 | tf_op jit(solution)/shard_map/all_to_all | solution.py:128
  238.3 11.5 copy-start.46
  252.0 40.3 %all-to-all-start.1 = ((bf16[8,4,29,768]{3,1,2,0:T(4,128)(2,1)}), bf16[8,4,29,768]{3,1,2,0:T(4,128)(2,1)}, u32[]{:S(2)}, u32[]{:S(2)}) async-start(bf16[8,4,29,768]{3,1,2,0:T(4,128)(2,1)} %copy.121), calls=%async_computation.1 | async-start | bytes 2850816 | tf_op jit(solution)/shard_map/all_to_all | solution.py:131
  271.3 11.5 copy-start.45
  282.8 15.0 %copy-start.40 = (s32[864]{0:T(1024)S(1)}, s32[864]{0:T(1024)}, u32[]{:S(2)}) copy-start(s32[864]{0:T(1024)} %copy-done.39) | copy-start | bytes 10372
  292.3 41.4 %all-to-all-start.3 = ((bf16[8,4,29,768]{3,1,2,0:T(4,128)(2,1)}), bf16[8,4,29,768]{3,1,2,0:T(4,128)(2,1)}, u32[]{:S(2)}, u32[]{:S(2)}) async-start(bf16[8,4,29,768]{3,1,2,0:T(4,128)(2,1)} %copy.126), calls=%async_computation.3 | async-start | bytes 2850816 | tf_op jit(solution)/shard_map/all_to_all | solution.py:131
  296.6 179.5 %reduce-scatter.3.cloned.1.call-start = ((), (), s32[]{:S(2)}) async-start(), calls=%async_computation.8 | async-start | bytes 6635520 | tf_op jit(solution)/shard_map/reduce_scatter | solution.py:282
  321.4 9.9 copy-start.22
  321.4 9.9 copy-start.30
  353.4 6.0 copy-start.20
  353.4 6.0 copy-start.24
  353.4 6.0 copy-start.26
  353.4 6.0 copy-start.28
  359.4 5.5 copy-start.4
  375.2 14.9 %copy-start.16 = (f32[3,12,144]{2,1,0:T(8,128)S(1)}, f32[3,12,144]{2,1,0:T(8,128)}, u32[]{:S(2)}) copy-start(f32[3,12,144]{2,1,0:T(8,128)} %log_add_fusion) | copy-start | bytes 62212
  390.1 9.9 copy-start.9
  412.1 127.4 %reduce-scatter.5.cloned.1.call-start = ((), (), s32[]{:S(2)}) async-start(), calls=%async_computation.9 | async-start | bytes 6635520 | tf_op jit(solution)/shard_map/reduce_scatter | solution.py:288
  429.7 763.5 %all-reduce.15.cloned.1.call-start = ((), (), s32[]{:S(2)}) async-start(), calls=%async_computation.11 | async-start | bytes 75497472 | tf_op jit(solution)/shard_map/psum | solution.py:327
  454.2 943.1 %all-reduce.13.cloned.1.call-start = ((), (), s32[]{:S(2)}) async-start(), calls=%async_computation.10 | async-start | bytes 19070976 | tf_op jit(solution)/shard_map/psum | solution.py:313
  551.5 5.5 copy-start.36
  551.5 5.5 copy-start.37
  1193.2 25.7 %copy-start.6 = (bf16[12288,768]{1,0:T(8,128)(2,1)S(1)}, bf16[12288,768]{1,0:T(8,128)(2,1)}, u32[]{:S(2)}) copy-start(bf16[12288,768]{1,0:T(8,128)(2,1)} %get-tuple-element.37) | copy-start | bytes 56623108
  1397.3 6.6 copy-start.14
  (25 other events, 60.7 us)
Sparse Core Ops, SparseCore 0:
  15.0 42.6 all-gather.4
  60.1 39.9 all-gather.2
  412.3 62.3 reduce-scatter.2
  477.5 61.9 reduce-scatter.4
  543.7 649.4 all-reduce.14
  1201.5 195.7 all-reduce.12
where the time goes:
time: 1420 us; the launch traced here: 1410 us
  waiting for transfers between devices  832 us (59%)
  local copies, waits for them, and re-layouts  215 us (15%)
  matrix products  178 us (13%)
  other arithmetic  110 us (8%)
  blocking collectives  40.4 us (3%)
  starting transfers between devices  20.5 us (1%)
  between operations  16.3 us (1%)
    psum x1, waiting for transfers between devices, per_device(): lax.psum(grad_first.astype(jnp.bfloat16), 'seq').astype(jnp.float32)  588 us
    psum x1, waiting for transfers between devices, per_device(): lax.psum((grad_qkv, grad_proj, grad_router, grad_gain_one, grad_shift_one...  165 us
    reduce_scatter x1, waiting for transfers between devices, per_device(): lax.psum_scatter(grad_values_full.reshape(image_count, full_patches, mode...  61.2 us
    psum x1, blocking collectives, per_device(): lax.psum((grad_qkv, grad_proj, grad_router, grad_gain_one, grad_shift_one...  40.4 us
    dot_general x1, matrix products, per_device(): jnp.einsum('secd,efd->secf', arrived, w_first, preferred_element_type=jnp...  35.2 us
  transfers between devices with their start and end apart: 10, of which 5 were waited for; matrix products, arithmetic and copies ran while one was open for 25% of the time, Pallas kernels for 0%

commit v1 on v0

--- a/solution.py
+++ b/solution.py
@@ -216,11 +216,19 @@
         "secd,efd->secf", grad_sent, w_second, preferred_element_type=jnp.float32
     )
     grad_pre = (grad_hidden * gelu_slope(pre_act)).astype(jnp.bfloat16)
+    rows_all = lax.all_gather(arrived, "seq", axis=0, tiled=True)
+    sent_all = lax.all_gather(grad_sent, "seq", axis=0, tiled=True)
+    pre_all = jnp.einsum("secd,efd->secf", rows_all, w_first, preferred_element_type=jnp.float32)
+    hidden_all = jax.nn.gelu(pre_all, approximate=False).astype(jnp.bfloat16)
+    grad_hidden_all = jnp.einsum(
+        "secd,efd->secf", sent_all, w_second, preferred_element_type=jnp.float32
+    )
+    grad_pre_all = (grad_hidden_all * gelu_slope(pre_all)).astype(jnp.bfloat16)
     grad_second = jnp.einsum(
-        "secf,secd->efd", hidden, grad_sent, preferred_element_type=jnp.float32
+        "secf,secd->efd", hidden_all, sent_all, preferred_element_type=jnp.float32
     ).reshape(-1, model_width)
     grad_first = jnp.einsum(
-        "secf,secd->efd", grad_pre, arrived, preferred_element_type=jnp.float32
+        "secf,secd->efd", grad_pre_all, rows_all, preferred_element_type=jnp.float32
     ).reshape(-1, model_width)
     grad_part_in = jnp.einsum(
         "secf,efd->secd", grad_pre, w_first, preferred_element_type=jnp.float32
@@ -310,11 +318,8 @@
         .astype(jnp.bfloat16)
         .reshape(image_count, patch_rows, model_width)
     )
-    summed = lax.psum(
+    small = lax.psum(
         (
-            grad_qkv,
-            grad_proj,
-            grad_router,
             grad_gain_one,
             grad_shift_one,
             grad_gain_two,
@@ -323,10 +328,12 @@
         ),
         ("seq", "ep"),
     )
-    expert_grads = (
-        lax.psum(grad_first.astype(jnp.bfloat16), "seq").astype(jnp.float32),
-        lax.psum(grad_second.astype(jnp.bfloat16), "seq").astype(jnp.float32),
-    )
+    big = lax.psum(
+        tuple(g.astype(jnp.bfloat16) for g in (grad_qkv, grad_proj, grad_router)),
+        ("seq", "ep"),
+    )
+    summed = tuple(g.astype(jnp.float32) for g in big) + small
+    expert_grads = (grad_first, grad_second)
     rms_stats = jnp.sqrt(summed[7][:3] / summed[7][3])
     return (
         output,

time: 1420 us -> 823 us (0.58)
  waiting for transfers between devices: 832 us -> 55.6 us
  matrix products: 178 us -> 347 us
  blocking collectives: 40.4 us -> 82.4 us
  other arithmetic: 110 us -> 84.3 us
    psum x2 -> x1, waiting for transfers between devices: 754 us -> 37.7 us  [per_device(): lax.psum(tuple((g.astype(jnp.bfloat16) for g in (grad_qkv, grad_proj, gra...]
    dot_general x3, matrix products: 38.1 us -> 200 us  [the longest x1 117 us: per_device(): jnp.einsum('secf,secd->efd', hidden_all, sent_all, preferred_element_type...]
    reduce_scatter x1, waiting for transfers between devices: 61.2 us -> 0.01 us  [per_device(): lax.psum_scatter(grad_values_full.reshape(image_count, full_patches, mode...]
    psum x1 -> x2, blocking collectives: 40.4 us -> 82.4 us  [the longest x1 41.6 us: per_device(): lax.psum((grad_gain_one, grad_shift_one, grad_gain_two, grad_shift_two, s...]
    convert_element_type x2 -> x3, other arithmetic: 34 us -> 8.59 us  [per_device(): summed = tuple((g.astype(jnp.float32) for g in big)) + small]
    dot_general x1, matrix products: 11.5 us -> 34.8 us  [per_device(): jnp.einsum('secf,efd->secd', hidden, w_second, preferred_element_type=jnp...]
    dot_general x1, matrix products: 35.2 us -> 12.2 us  [per_device(): jnp.einsum('secd,efd->secf', arrived, w_first, preferred_element_type=jnp...]
  transfers between devices with their start and end apart: 10 -> 11, of which waited for: 5 -> 3; matrix products, arithmetic and copies ran while one was open for 25% -> 70% of each run, Pallas kernels for 0% -> 0%
where the time goes in v1:
time: 823 us; the launch traced here: 815 us
  matrix products  347 us (42%)
  local copies, waits for them, and re-layouts  210 us (26%)
  other arithmetic  84.3 us (10%)
  blocking collectives  82.4 us (10%)
  waiting for transfers between devices  55.6 us (7%)
  starting transfers between devices  20.2 us (2%)
  between operations  16.3 us (2%)
    dot_general x1, matrix products, per_device(): jnp.einsum('secf,secd->efd', hidden_all, sent_all, preferred_element_type...  117 us
    dot_general x1, matrix products, per_device(): jnp.einsum('secf,secd->efd', grad_pre_all, rows_all, preferred_element_ty...  53 us
    psum x1, blocking collectives, per_device(): lax.psum((grad_gain_one, grad_shift_one, grad_gain_two, grad_shift_two, s...  41.6 us
    psum x1, blocking collectives, per_device(): lax.psum(tuple((g.astype(jnp.bfloat16) for g in (grad_qkv, grad_proj, gra...  40.8 us
    psum x1, waiting for transfers between devices, per_device(): lax.psum(tuple((g.astype(jnp.bfloat16) for g in (grad_qkv, grad_proj, gra...  37.7 us
    dot_general x1, matrix products, per_device(): jnp.einsum('secf,efd->secd', hidden, w_second, preferred_element_type=jnp...  34.8 us
    dot_general x1, matrix products, per_device(): jnp.einsum('secd,efd->secf', rows_all, w_first, preferred_element_type=jn...  29.5 us
    dot_general x1, matrix products, per_device(): jnp.einsum('secf,efd->secd', grad_pre, w_first, preferred_element_type=jn...  20.4 us
  transfers between devices with their start and end apart: 11, of which 3 were waited for; matrix products, arithmetic and copies ran while one was open for 70% of the time, Pallas kernels for 0%

profile of v1, /device:TPU:0, one launch (start us, length us, event | category | flops | bytes accessed | tf_op | source)
XLA Modules:
  0.0 815.0 jit_solution(9045719646256218311)
XLA Ops:
  28.5 6.5 gather_fusion
  35.1 7.7 gather_fusion.1
  65.3 5.5 scatter_custom_fusion.1
  71.6 5.4 copy.140
  90.7 9.3 %all-gather.5.cloned.1.call-done = bf16[3,576,768]{2,1,0:T(8,128)(2,1)} async-done(((bf16[3,144,768]{2,1,0:T(8,128)(2,1)}), bf16[3,576,768]{2,1,0:T(8,128)(2,1)}) %all-gather.5.cloned.1.call-update) | async-done | bytes 2654224 | tf_op jit(solution)/shard_map/all_gather | solution.py:154
  105.3 8.2 %fusion.72 = bf16[3,144,12,64]{1,3,2,0:T(8,128)(2,1)} fusion(bf16[3,576,12,64]{1,3,2,0:T(8,128)(2,1)} %bitcast.270, f32[3,12,144,576]{3,2,1,0:T(8,128)} %copy-done.1, f32[3,12,144]{2,1,0:T(8,128)} %fusion.48, f32[3,12,144]{2,1,0:T(8,128)} %copy-done.18), kind=kOutput, calls=%fused_computation.118 | convolution fusion | flops 391495680 | bytes 15303168 | tf_op jit(solution)/shard_map/ihst,ithd->ishd/dot_general | solution.py:163
  128.0 6.7 gather_fusion.4
  160.9 5.4 scatter_custom_fusion.2
  169.6 12.0 %gather_fusion.8 = f32[864]{0:T(1024)S(1)} fusion(f32[432,32]{0,1:T(8,128)} %fusion.83, s32[864]{0:T(1024)S(1)} %reshape.493), kind=kCustom, calls=%fused_computation.8 | custom fusion | bytes 13824 | tf_op jit(solution)/shard_map/jit(take_along_axis)/gather | solution.py:194
  184.8 7.0 gather_fusion.6
  205.9 12.2 %fusion.63 = f32[4,8,29,3072]{3,2,1,0:T(8,128)} fusion(bf16[4,3072,768,1]{2,1,3,0:T(8,128)(2,1)} %bitcast.267, bf16[8,4,29,768]{3,1,2,0:T(4,128)(2,1)} %all-to-all-done), kind=kOutput, calls=%fused_computation.109 | convolution fusion | flops 4378853376 | bytes 31703040 | tf_op jit(solution)/shard_map/secd,efd->secf/dot_general | solution.py:186
  218.2 34.8 %fusion.69 = bf16[8,4,29,768]{3,2,0,1:T(8,128)(2,1)S(1)} fusion(bf16[4,3072,768,1]{2,1,3,0:T(8,128)(2,1)} %bitcast.283, f32[4,8,29,3072]{3,2,1,0:T(8,128)} %fusion.63), kind=kOutput, calls=%fused_computation.114 | convolution fusion | flops 4564869120 | bytes 31703040 | tf_op jit(solution)/shard_map/secf,efd->secd/dot_general | solution.py:188
  263.2 20.4 %fusion.66 = bf16[8,4,29,768]{3,2,0,1:T(8,128)(2,1)} fusion(bf16[4,3072,768,1]{2,1,3,0:T(8,128)(2,1)} %bitcast.268, f32[4,8,29,3072]{3,2,1,0:T(8,128)} %fusion.63, bf16[4,3072,768,1]{2,1,3,0:T(8,128)(2,1)} %bitcast.284, bf16[8,4,29,768]{3,1,2,0:T(4,128)(2,1)} %all-to-all-done.2), kind=kOutput, calls=%fused_computation.113 | convolution fusion | flops 8786927616 | bytes 52002816 | tf_op jit(solution)/shard_map/secf,efd->secd/dot_general | solution.py:233
  287.2 7.8 all-to-all-done.1
  313.9 6.6 gather_fusion.5
  325.0 7.5 multiply_reduce_fusion.1
  342.5 6.6 gather_fusion.7
  354.0 6.0 reduce_sum.241
  378.4 14.9 %multiply_reduce_fusion = (f32[3,12,144]{2,1,0:T(8,128)S(1)}, f32[3,12,144,576]{3,2,1,0:T(8,128)}) fusion(f32[3,12,144,576]{3,2,1,0:T(8,128)} %copy-done.1, f32[3,12,144]{2,1,0:T(8,128)} %log_add_fusion, bf16[3,144,12,64]{1,3,2,0:T(8,128)(2,1)} %copy.160, bf16[3,576,12,64]{1,3,2,0:T(8,128)(2,1)} %bitcast.271), kind=kOutput, calls=%fused_computation.50 | convolution fusion | flops 391158720 | bytes 27247104 | tf_op jit(solution)/shard_map/ishd,ithd->ihst/dot_general | solution.py:270
  393.3 9.9 %multiply_convert_fusion = bf16[3,12,144,576]{3,2,1,0:T(8,128)(2,1)S(1)} fusion(f32[3,12,144,576]{3,2,1,0:T(8,128)} %get-tuple-element.53, f32[3,12,144,576]{3,2,1,0:T(8,128)} %copy-done.1, f32[3,12,144]{2,1,0:T(8,128)S(1)} %get-tuple-element.52, f32[3,12,144]{2,1,0:T(8,128)S(1)} %copy-done.15), kind=kLoop, calls=%fused_computation.49 | loop fusion | flops 11943936 | bytes 29901312 | tf_op jit(solution)/shard_map/convert_element_type | solution.py:274
  407.8 7.5 copy.163
  416.0 7.5 fusion.73
  431.1 10.3 %fusion.50 = f32[3,12,64,576]{3,2,1,0:T(8,128)} fusion(bf16[3,144,12,64]{1,3,2,0:T(8,128)(2,1)} %copy.160, f32[3,12,144,576]{3,2,1,0:T(8,128)} %copy-done.1, f32[3,12,144]{2,1,0:T(8,128)} %log_add_fusion), kind=kOutput, calls=%fused_computation.89 | convolution fusion | flops 388177920 | bytes 17936640 | tf_op jit(solution)/shard_map/ihst,ishd->ithd/dot_general | solution.py:283
  441.4 7.5 copy.165
  450.8 40.8 %psum.62 = bf16[768,32]{0,1:T(8,128)(2,1)} all-reduce(bf16[768,32]{0,1:T(8,128)(2,1)} %convolution_convert_fusion.4), channel_id=1, replica_groups=mesh['seq'=4,'ep'=8] {'seq','ep'}, use_global_device_ids=true, to_apply=%region_36.37 | all-reduce | flops 24576 | bytes 98304 | tf_op jit(solution)/shard_map/psum | solution.py:331
  499.0 29.5 %fusion.169 = f32[4,32,29,3072]{3,1,2,0:T(8,128)} fusion(bf16[32,4,29,768]{3,0,2,1:T(8,128)(2,1)} %all-gather.11.cloned.1.call-done, bf16[4,3072,768,1]{2,1,3,0:T(8,128)(2,1)} %bitcast.269), kind=kOutput, calls=%fused_computation.287 | convolution fusion | flops 17515413504 | bytes 70189056 | tf_op jit(solution)/shard_map/secd,efd->secf/dot_general | solution.py:221
  528.4 117.1 %fusion.23 = f32[4,3072,768,1]{2,1,3,0:T(8,128)} fusion(bf16[32,4,29,768]{3,0,2,1:T(8,128)(2,1)} %all-gather.9.cloned.1.call-done, f32[4,32,29,3072]{3,1,2,0:T(8,128)} %fusion.169), kind=kOutput, calls=%fused_computation.46 | convolution fusion | flops 18256625664 | bytes 89063424 | tf_op jit(solution)/shard_map/secf,secd->efd/dot_general | solution.py:227
  655.4 53.0 %fusion.170 = f32[4,3072,768,1]{2,1,3,0:T(8,128)} fusion(bf16[32,4,29,768]{3,0,2,1:T(8,128)(2,1)} %all-gather.11.cloned.1.call-done, f32[4,32,29,3072]{3,1,2,0:T(8,128)} %fusion.169, bf16[32,4,29,768]{3,0,2,1:T(8,128)(2,1)} %all-gather.9.cloned.1.call-done, bf16[4,3072,768,1]{2,1,3,0:T(8,128)(2,1)} %bitcast.285), kind=kOutput, calls=%fused_computation.288 | convolution fusion | flops 35144859648 | bytes 113639424 | tf_op jit(solution)/shard_map/secf,secd->efd/dot_general | solution.py:230
  708.4 5.5 multiply_reduce_fusion.4
  713.9 41.6 %all-reduce.7 = (f32[768]{0:T(1024)}, f32[768]{0:T(1024)}, f32[768]{0:T(1024)}, f32[768]{0:T(1024)}, f32[4]{0:T(128)}) all-reduce(f32[768]{0:T(1024)} %get-tuple-element.17, f32[768]{0:T(1024)} %get-tuple-element.26, f32[768]{0:T(1024)S(1)} %copy-done.36, f32[768]{0:T(1024)S(1)} %copy-done.37, ...), channel_id=1, replica_groups=mesh['seq'=4,'ep'=8] {'seq','ep'}, use_global_device_ids=true, to_apply=%region_27.28 | all-reduce | flops 3076 | bytes 24608 | tf_op jit(solution)/shard_map/psum | solution.py:321
  763.1 37.7 %all-reduce.11.cloned.1.call-done = (bf16[768,2304]{1,0:T(8,128)(2,1)}, bf16[768,768]{1,0:T(8,128)(2,1)}) async-done(((bf16[768,2304]{1,0:T(8,128)(2,1)}, bf16[768,768]{1,0:T(8,128)(2,1)}), (bf16[768,2304]{1,0:T(8,128)(2,1)}, bf16[768,768]{1,0:T(8,128)(2,1)})) %all-reduce.11.cloned.1.call-update) | async-done | bytes 4718608 | tf_op jit(solution)/shard_map/psum | solution.py:331
  800.8 5.6 convert_element_type.154
  (237 shorter events, 234.9 us)
Async XLA Ops:
  7.2 64.4 %all-gather.7.cloned.1.call-start = ((), (), s32[]{:S(2)}) async-start(), calls=%async_computation.7 | async-start | bytes 3317760 | tf_op jit(solution)/shard_map/all_gather | solution.py:153
  13.5 10.4 %copy-start.31 = (s32[3,144,2]{1,2,0:T(2,128)S(1)}, s32[3,144,2]{1,2,0:T(2,128)}, u32[]{:S(2)}) copy-start(s32[3,144,2]{1,2,0:T(2,128)} %param.15) | copy-start | bytes 10372
  13.5 11.2 %copy-start.44 = (s32[3,144]{1,0:T(4,128)S(1)}, s32[3,144]{1,0:T(4,128)}, u32[]{:S(2)}) copy-start(s32[3,144]{1,0:T(4,128)} %param.16) | copy-start | bytes 5188
  14.9 85.1 %all-gather.5.cloned.1.call-start = ((), (), s32[]{:S(2)}) async-start(), calls=%async_computation.6 | async-start | bytes 3317760 | tf_op jit(solution)/shard_map/all_gather | solution.py:154
  113.6 12.1 %copy-start.24 = (f32[768]{0:T(1024)S(1)}, f32[768]{0:T(1024)}, u32[]{:S(2)}) copy-start(f32[768]{0:T(1024)} %param.22) | copy-start | bytes 9220
  113.6 12.1 %copy-start.42 = (f32[768]{0:T(1024)S(1)}, f32[768]{0:T(1024)}, u32[]{:S(2)}) copy-start(f32[768]{0:T(1024)} %param.23) | copy-start | bytes 9220
  140.8 57.1 %all-to-all-start = ((bf16[8,4,29,768]{3,1,2,0:T(4,128)(2,1)}), bf16[8,4,29,768]{3,1,2,0:T(4,128)(2,1)}, u32[]{:S(2)}, u32[]{:S(2)}) async-start(bf16[8,4,29,768]{3,1,2,0:T(4,128)(2,1)} %copy.149), calls=%async_computation | async-start | bytes 2850816 | tf_op jit(solution)/shard_map/all_to_all | solution.py:128
  146.6 21.2 %copy-start.26 = (f32[432]{0:T(512)}, f32[432]{0:T(512)S(1)}, u32[]{:S(2)}) copy-start(f32[432]{0:T(512)S(1)} %convert_element_type.139) | copy-start | bytes 5188
  169.6 12.0 %copy-start.38 = (s32[864]{0:T(1024)S(1)}, s32[864]{0:T(1024)}, u32[]{:S(2)}) copy-start(s32[864]{0:T(1024)} %reshape.418) | copy-start | bytes 10372
  181.7 10.2 %copy-start.5 = (f32[864]{0:T(1024)}, f32[864]{0:T(1024)S(1)}, u32[]{:S(2)}) copy-start(f32[864]{0:T(1024)S(1)} %gather_fusion.8) | copy-start | bytes 10372
  197.9 57.2 %all-to-all-start.2 = ((bf16[8,4,29,768]{3,1,2,0:T(4,128)(2,1)}), bf16[8,4,29,768]{3,1,2,0:T(4,128)(2,1)}, u32[]{:S(2)}, u32[]{:S(2)}) async-start(bf16[8,4,29,768]{3,1,2,0:T(4,128)(2,1)} %copy.154), calls=%async_computation.2 | async-start | bytes 2850816 | tf_op jit(solution)/shard_map/all_to_all | solution.py:128
  203.0 295.9 %all-gather.11.cloned.1.call-start = ((), (), s32[]{:S(2)}) async-start(), calls=%async_computation.11 | async-start | bytes 7127040 | tf_op jit(solution)/shard_map/all_gather | solution.py:219
  255.2 39.8 %all-to-all-start.1 = ((bf16[8,4,29,768]{3,1,2,0:T(4,128)(2,1)}), bf16[8,4,29,768]{3,1,2,0:T(4,128)(2,1)}, u32[]{:S(2)}, u32[]{:S(2)}) async-start(bf16[8,4,29,768]{3,1,2,0:T(4,128)(2,1)} %copy.151), calls=%async_computation.1 | async-start | bytes 2850816 | tf_op jit(solution)/shard_map/all_to_all | solution.py:131
  260.2 268.2 %all-gather.9.cloned.1.call-start = ((), (), s32[]{:S(2)}) async-start(), calls=%async_computation.10 | async-start | bytes 7127040 | tf_op jit(solution)/shard_map/all_gather | solution.py:220
  263.2 37.8 %copy-start.40 = (s32[864]{0:T(1024)S(1)}, s32[864]{0:T(1024)}, u32[]{:S(2)}) copy-start(s32[864]{0:T(1024)} %copy-done.39) | copy-start | bytes 10372
  263.2 37.8 %copy-start.6 = (f32[864]{0:T(1024)S(1)}, f32[864]{0:T(1024)}, u32[]{:S(2)}) copy-start(f32[864]{0:T(1024)} %copy-done.5) | copy-start | bytes 10372
  295.0 39.1 %all-to-all-start.3 = ((bf16[8,4,29,768]{3,1,2,0:T(4,128)(2,1)}), bf16[8,4,29,768]{3,1,2,0:T(4,128)(2,1)}, u32[]{:S(2)}, u32[]{:S(2)}) async-start(bf16[8,4,29,768]{3,1,2,0:T(4,128)(2,1)} %copy.156), calls=%async_computation.3 | async-start | bytes 2850816 | tf_op jit(solution)/shard_map/all_to_all | solution.py:131
  299.3 346.2 %reduce-scatter.3.cloned.1.call-start = ((), (), s32[]{:S(2)}) async-start(), calls=%async_computation.8 | async-start | bytes 6635520 | tf_op jit(solution)/shard_map/reduce_scatter | solution.py:290
  349.1 11.7 %copy-start.23 = (f32[432]{0:T(512)S(1)}, f32[432]{0:T(512)}, u32[]{:S(2)}) copy-start(f32[432]{0:T(512)} %copy-done.22) | copy-start | bytes 5188
  349.1 13.6 %copy-start.21 = (f32[432]{0:T(512)S(1)}, f32[432]{0:T(512)}, u32[]{:S(2)}) copy-start(f32[432]{0:T(512)} %copy-done.20) | copy-start | bytes 5188
  349.2 13.6 %copy-start.25 = (f32[768]{0:T(1024)S(1)}, f32[768]{0:T(1024)}, u32[]{:S(2)}) copy-start(f32[768]{0:T(1024)} %param.22) | copy-start | bytes 9220
  349.2 13.6 %copy-start.27 = (f32[432]{0:T(512)S(1)}, f32[432]{0:T(512)}, u32[]{:S(2)}) copy-start(f32[432]{0:T(512)} %copy-done.26) | copy-start | bytes 5188
  360.0 8.1 copy-start.4
  360.0 8.1 copy-start.12
  360.0 8.1 copy-start.29
  360.0 9.7 %copy-start.11 = (bf16[768,768]{1,0:T(8,128)(2,1)S(1)}, bf16[768,768]{1,0:T(8,128)(2,1)}, u32[]{:S(2)}) copy-start(bf16[768,768]{1,0:T(8,128)(2,1)} %param.21) | copy-start | bytes 3538948
  378.4 14.9 %copy-start.15 = (f32[3,12,144]{2,1,0:T(8,128)S(1)}, f32[3,12,144]{2,1,0:T(8,128)}, u32[]{:S(2)}) copy-start(f32[3,12,144]{2,1,0:T(8,128)} %log_add_fusion) | copy-start | bytes 62212
  393.3 9.9 %copy-start.10 = (bf16[3,144,12,64]{1,3,2,0:T(8,128)(2,1)S(1)}, bf16[3,144,12,64]{1,3,2,0:T(8,128)(2,1)}, u32[]{:S(2)}) copy-start(bf16[3,144,12,64]{1,3,2,0:T(8,128)(2,1)} %copy.141) | copy-start | bytes 1990660
  415.3 232.5 %reduce-scatter.5.cloned.1.call-start = ((), (), s32[]{:S(2)}) async-start(), calls=%async_computation.9 | async-start | bytes 6635520 | tf_op jit(solution)/shard_map/reduce_scatter | solution.py:296
  496.5 304.3 %all-reduce.11.cloned.1.call-start = ((), (), s32[]{:S(2)}) async-start(), calls=%async_computation.12 | async-start | bytes 9437184 | tf_op jit(solution)/shard_map/psum | solution.py:331
  655.4 53.0 %copy-start.33 = (f32[432]{0:T(512)S(1)}, f32[432]{0:T(512)}, u32[]{:S(2)}) copy-start(f32[432]{0:T(512)} %copy-done.32) | copy-start | bytes 5188
  655.4 53.0 %copy-start.35 = (f32[432]{0:T(512)S(1)}, f32[432]{0:T(512)}, u32[]{:S(2)}) copy-start(f32[432]{0:T(512)} %copy-done.34) | copy-start | bytes 5188
  (24 other events, 68.4 us)
Sparse Core Ops, SparseCore 0:
  15.0 42.6 all-gather.6
  60.1 39.9 all-gather.4
  206.1 65.7 all-gather.10
  273.5 65.2 all-gather.8
  415.4 62.4 reduce-scatter.2
  496.6 62.5 reduce-scatter.4
  655.5 145.2 all-reduce.10
